TPU v7x, 256 devices: a whole 4x4x8 slice. The times are simulated.
256 devices in a mesh: firm: 16 (over y_lo, z), tm: 16 (over x, y_hi, core).
Axes of the slice: x: 4, y: 4 (y_hi: 2, y_lo: 2; y = y_hi * 2 + y_lo), z: 8, core: 2. Of those that a mesh axis runs over, the one named last changes fastest.
Arguments:
- features: bfloat16 [8192, 32, 128], P('firm', 'tm'), may hold values from -6 to 6
- cotangent: bfloat16 [8192, 32, 128], P('firm', 'tm'), may hold values from -6 to 6
- tiles: bfloat16 [64, 64, 128, 128], P('firm'), may hold values from -0.125 to 0.125
- mask: int32 [64, 64], P('firm'), may hold values 0 or 1
- w_prev: bfloat16 [2, 128, 256], replicated, may hold values from -0.375 to 0.375
- w_cur: bfloat16 [2, 128, 256], replicated, may hold values from -0.375 to 0.375
- w_self: bfloat16 [2, 128, 128], replicated, may hold values from -0.5 to 0.5
- w_nbr: bfloat16 [2, 128, 128], replicated, may hold values from -0.5 to 0.5
- dilations: int32 [2], replicated, may hold values from 1 to 2, as said below
Outputs:
- grad_features: float32 [8192, 32, 128], P('firm', 'tm')
- grad_prev: float32 [2, 128, 256], replicated
- grad_cur: float32 [2, 128, 256], replicated
- grad_self: float32 [2, 128, 128], replicated
- grad_nbr: float32 [2, 128, 128], replicated
Inputs may be any that keep to these rules, and one draw needn't show every extreme that they name: `dilations`: each layer's dilation lies between 1 and 2; some layer has dilation 1 and some layer has dilation 2.
All inputs are finite; a program needn't handle non-finite values. No bound on the sum of `mask` on one device may be relied on, other than what follows from the above.
Results may differ from a plain program's by a relative error of at most 0.007.
Values may be sent and summed in bfloat16 or wider, within the bound.
No kernel may reach another device: no remote copies, remote signals or barrier semaphores. Data moves between devices by JAX's collectives and lax.ppermute only.
A program may use at most 128 MiB of HBM per device.

v0:
```python
import jax
import jax.numpy as jnp
from jax import lax
from jax.sharding import PartitionSpec as P

L = 2


def shifted(array, axis, by):
    peers = lax.axis_size(axis)
    pairs = [(i, i + by) for i in range(peers) if 0 <= i + by < peers]
    return lax.ppermute(array, axis, pairs)


def earlier_time_days(hidden_state, dilation_factor):
    time_days = hidden_state.shape[1]
    prior = shifted(hidden_state, "tm", 1)
    paired_terms = jnp.concatenate([prior, hidden_state], axis=1)
    return lax.dynamic_slice_in_dim(paired_terms, time_days - dilation_factor, time_days, 1)


def later_time_days(reverse_flow, dilation_factor):
    time_days = reverse_flow.shape[1]
    following = shifted(reverse_flow, "tm", -1)
    paired_terms = jnp.concatenate([reverse_flow, following], axis=1)
    return lax.dynamic_slice_in_dim(paired_terms, dilation_factor, time_days, 1)


def folder(matrix, piece):
    return jnp.dot(matrix, piece, preferred_element_type=jnp.float32)


def per_device(features, cotangent, tiles, mask, w_prev, w_cur, w_self, w_nbr, dilations):
    rows, time_days, width = features.shape
    blocks_local, blocks_all, block_size, _ = tiles.shape
    all_firms = blocks_all * block_size
    masked = tiles * mask.astype(tiles.dtype)[:, :, None, None]
    row_matrix = masked.transpose(0, 2, 1, 3).reshape(rows, all_firms)
    saved = []
    hidden_state = features
    for layer_index in range(L):
        dilation_factor = dilations[layer_index]
        previous_state = earlier_time_days(hidden_state, dilation_factor)
        pre = jnp.dot(
            previous_state.reshape(-1, width),
            w_prev[layer_index],
            preferred_element_type=jnp.float32,
        )
        pre = pre + jnp.dot(
            hidden_state.reshape(-1, width), w_cur[layer_index], preferred_element_type=jnp.float32
        )
        filt = pre[:, :width]
        gate = pre[:, width:]
        gated = (jnp.tanh(filt) * jax.nn.sigmoid(gate)).astype(jnp.bfloat16)
        diffused = folder(
            row_matrix,
            lax.all_gather(gated.reshape(rows, time_days * width), "firm", axis=0, tiled=True),
        ).astype(jnp.bfloat16)
        mixed = jnp.dot(gated, w_self[layer_index], preferred_element_type=jnp.float32)
        mixed = mixed + jnp.dot(
            diffused.reshape(-1, width), w_nbr[layer_index], preferred_element_type=jnp.float32
        )
        saved.append((hidden_state, previous_state, filt, gate, gated, diffused))
        hidden_state = (
            hidden_state.astype(jnp.float32) + mixed.reshape(rows, time_days, width)
        ).astype(jnp.bfloat16)
    gradient_value = cotangent.astype(jnp.float32)
    outs_prev, outs_cur, outs_self, outs_nbr = ([], [], [], [])
    for layer_index in reversed(range(L)):
        hidden_state, previous_state, filt, gate, gated, diffused = saved[layer_index]
        dilation_factor = dilations[layer_index]
        gzb = gradient_value.astype(jnp.bfloat16).reshape(-1, width)
        outs_self.append(jnp.dot(gated.T, gzb, preferred_element_type=jnp.float32))
        outs_nbr.append(
            jnp.dot(diffused.reshape(-1, width).T, gzb, preferred_element_type=jnp.float32)
        )
        gdiff = jnp.dot(gzb, w_nbr[layer_index].T, preferred_element_type=jnp.float32).astype(
            jnp.bfloat16
        )
        gdiff_rows = gdiff.reshape(rows, time_days * width)
        spread = lax.psum_scatter(
            lax.dot_general(
                row_matrix, gdiff_rows, (((0,), (0,)), ((), ())), preferred_element_type=jnp.float32
            ),
            "firm",
            scatter_dimension=0,
            tiled=True,
        )
        ggated = jnp.dot(
            gzb, w_self[layer_index].T, preferred_element_type=jnp.float32
        ) + spread.reshape(-1, width)
        tanh_filt = jnp.tanh(filt)
        sig_gate = jax.nn.sigmoid(gate)
        gpre = jnp.concatenate(
            [
                ggated * sig_gate * (1.0 - tanh_filt * tanh_filt),
                ggated * tanh_filt * sig_gate * (1.0 - sig_gate),
            ],
            axis=1,
        ).astype(jnp.bfloat16)
        outs_cur.append(
            jnp.dot(hidden_state.reshape(-1, width).T, gpre, preferred_element_type=jnp.float32)
        )
        outs_prev.append(
            jnp.dot(previous_state.reshape(-1, width).T, gpre, preferred_element_type=jnp.float32)
        )
        reverse_flow = jnp.dot(
            gpre, w_prev[layer_index].T, preferred_element_type=jnp.float32
        ).reshape(rows, time_days, width)
        direct_path = jnp.dot(
            gpre, w_cur[layer_index].T, preferred_element_type=jnp.float32
        ).reshape(rows, time_days, width)
        gradient_value = (
            gradient_value + direct_path + later_time_days(reverse_flow, dilation_factor)
        )
    sums = lax.psum(
        (
            jnp.stack(outs_prev[::-1]),
            jnp.stack(outs_cur[::-1]),
            jnp.stack(outs_self[::-1]),
            jnp.stack(outs_nbr[::-1]),
        ),
        ("firm", "tm"),
    )
    factor = 1.0 / jnp.sqrt(jnp.float32(all_firms * time_days * lax.axis_size("tm")))
    return (gradient_value, sums[0] * factor, sums[1] * factor, sums[2] * factor, sums[3] * factor)


def solution(mesh):
    in_specs = (
        P("firm", "tm", None),
        P("firm", "tm", None),
        P("firm", None, None, None),
        P("firm", None),
        P(),
        P(),
        P(),
        P(),
        P(),
    )
    out_specs = (P("firm", "tm", None), P(), P(), P(), P())
    return jax.shard_map(
        per_device, mesh=mesh, in_specs=in_specs, out_specs=out_specs, check_vma=False
    )
```

profile of v0, /device:TPU:97, one launch (start us, length us, event | category | flops | bytes accessed | tf_op | source)
XLA Modules:
  0.0 658.3 jit_solution(12701526937728373321)
XLA Ops:
  7.2 5.4 collective-permute-start
  16.4 1.9 fusion.29
  21.3 7.2 %multiply_bitcast_fusion = bf16[4,128,64,128]{3,1,2,0:T(8,128)(2,1)} fusion(bf16[4,64,128,128]{3,2,1,0:T(8,128)(2,1)} %param.11, bf16[4,64]{1,0:T(4,128)(2,1)S(1)} %convert_element_type.41), kind=kLoop, calls=%fused_computation.8 | loop fusion | flops 4194304 | bytes 16777728 | tf_op jit(solution)/shard_map/transpose | solution.py:38
  28.6 12.1 %copy.22 = bf16[4,128,64,128]{3,2,1,0:T(8,128)(2,1)} copy(bf16[4,128,64,128]{3,1,2,0:T(8,128)(2,1)} %multiply_bitcast_fusion) | data formatting | bytes 16777216 | tf_op jit(solution)/shard_map/transpose | solution.py:38
  41.0 24.6 %fusion.6 = f32[8192,256]{1,0:T(8,128)} fusion(bf16[512,256]{1,0:T(8,128)(2,1)S(1)} %reshape.86, bf16[64,8,64,128]{3,2,1,0:T(8,128)(2,1)} %bitcast.124), kind=kOutput, calls=%fused_computation.6 | convolution fusion | flops 2147483648 | bytes 17039360 | tf_op jit(solution)/shard_map/dot_general | solution.py:82
  66.7 19.3 %all-gather.3.cloned.1.call-done = bf16[8192,256]{1,0:T(8,128)(2,1)} async-done(((bf16[512,256]{1,0:T(8,128)(2,1)}), bf16[8192,256]{1,0:T(8,128)(2,1)}) %all-gather.3.cloned.1.call-update) | async-done | bytes 4194320 | tf_op jit(solution)/shard_map/all_gather | solution.py:57
  86.1 9.3 %fusion.13 = bf16[512,256]{1,0:T(8,128)(2,1)S(1)} fusion(bf16[8192,256]{1,0:T(8,128)(2,1)} %all-gather.3.cloned.1.call-done, bf16[64,8,64,128]{3,2,1,0:T(8,128)(2,1)} %bitcast.125), kind=kOutput, calls=%fused_computation.23 | convolution fusion | flops 2147614720 | bytes 12845056 | tf_op jit(solution)/shard_map/dot_general | solution.py:30
  95.9 14.7 %collective-permute-start.1 = (bf16[512,2,128]{2,1,0:T(2,128)(2,1)S(1)}, bf16[512,2,128]{2,1,0:T(2,128)(2,1)S(1)}, u32[]{:S(2)}, u32[]{:S(2)}) collective-permute-start(bf16[512,2,128]{2,1,0:T(2,128)(2,1)S(1)} %add_convert_fusion), channel_id=1, source_target_pairs={{0,1},{1,2},{2,3},{3,4},{4,5},{5,6},{6,7},{7,8},{8,9},{9,10},{10,1... | collective-permute-start | bytes 786440 | tf_op jit(solution)/shard_map/ppermute | solution.py:12
  116.0 82.7 %reduce-scatter.3.cloned.1.call-done = f32[512,256]{1,0:T(8,128)} async-done(((f32[8192,256]{1,0:T(8,128)}), f32[512,256]{1,0:T(8,128)}) %reduce-scatter.3.cloned.1.call-update) | async-done | bytes 524304 | tf_op jit(solution)/shard_map/reduce_scatter | solution.py:81
  198.7 1.9 reshape.87
  200.6 2.4 multiply_convert_fusion.3
  202.9 1.8 reshape.98
  207.1 2.8 collective-permute-start.2
  211.9 7.5 %collective-permute-done.2 = f32[512,2,128]{2,0,1:T(8,128)} collective-permute-done((f32[512,2,128]{2,0,1:T(8,128)S(1)}, f32[512,2,128]{2,0,1:T(8,128)}, u32[]{:S(2)}, u32[]{:S(2)}) %collective-permute-start.2) | collective-permute-done | bytes 524320 | tf_op jit(solution)/shard_map/ppermute | solution.py:12
  219.3 2.2 fusion.68
  222.9 24.2 %fusion.2 = f32[8192,256]{1,0:T(8,128)} fusion(bf16[512,256]{1,0:T(8,128)(2,1)S(1)} %reshape.96, bf16[64,8,64,128]{3,2,1,0:T(8,128)(2,1)} %bitcast.126), kind=kOutput, calls=%fused_computation.2 | convolution fusion | flops 2147483648 | bytes 17039360 | tf_op jit(solution)/shard_map/dot_general | solution.py:82
  248.3 1.9 convolution_bitcast_fusion
  250.2 1.9 convolution_bitcast_fusion.2
  253.3 16.1 %all-gather.5.cloned.1.call-done = bf16[8192,256]{1,0:T(8,128)(2,1)} async-done(((bf16[512,256]{1,0:T(8,128)(2,1)}), bf16[8192,256]{1,0:T(8,128)(2,1)}) %all-gather.5.cloned.1.call-update) | async-done | bytes 4194320 | tf_op jit(solution)/shard_map/all_gather | solution.py:57
  269.4 9.3 %fusion.16 = bf16[512,256]{1,0:T(8,128)(2,1)S(1)} fusion(bf16[8192,256]{1,0:T(8,128)(2,1)} %all-gather.5.cloned.1.call-done, bf16[64,8,64,128]{3,2,1,0:T(8,128)(2,1)} %bitcast.127), kind=kOutput, calls=%fused_computation.24 | convolution fusion | flops 2147614720 | bytes 12845056 | tf_op jit(solution)/shard_map/dot_general | solution.py:30
  279.7 101.9 %reduce-scatter.5.cloned.1.call-done = f32[512,256]{1,0:T(8,128)} async-done(((f32[8192,256]{1,0:T(8,128)}), f32[512,256]{1,0:T(8,128)}) %reduce-scatter.5.cloned.1.call-update) | async-done | bytes 524304 | tf_op jit(solution)/shard_map/reduce_scatter | solution.py:81
  387.2 2.7 collective-permute-start.3
  391.8 254.4 %all-reduce.3.cloned.1.call-done = (f32[2,128,256]{2,1,0:T(8,128)}, f32[2,128,256]{2,1,0:T(8,128)}, f32[2,128,128]{2,1,0:T(8,128)}, f32[2,128,128]{2,1,0:T(8,128)}) async-done(((f32[2,128,256]{2,1,0:T(8,128)}, f32[2,128,256]{2,1,0:T(8,128)}, f32[2,128,128]{2,1,0:T(8,128)}, f32[2,128,128]{2,1,0:T(8,128)}), (f32[2,128,256]{2,1,0:T(8,128)}, f32[2,128,256]{2,1,0:T(8,128)}, f32[2,128,128]{2,1,0:T(8,128)}, ...) | async-done | bytes 786448 | tf_op jit(solution)/shard_map/psum | solution.py:116
  647.9 1.9 broadcast_multiply_fusion
  (83 shorter events, 27.3 us)
Async XLA Ops:
  7.2 78.9 %all-gather.3.cloned.1.call-start = ((), (), s32[]{:S(2)}) async-start(), calls=%async_computation.3 | async-start | bytes 4456448 | tf_op jit(solution)/shard_map/all_gather | solution.py:57
  7.2 9.2 %collective-permute-start = (bf16[512,2,128]{2,1,0:T(2,128)(2,1)}, bf16[512,2,128]{2,1,0:T(2,128)(2,1)S(1)}, u32[]{:S(2)}, u32[]{:S(2)}) collective-permute-start(bf16[512,2,128]{2,1,0:T(2,128)(2,1)} %param.9), channel_id=1, source_target_pairs={{0,1},{1,2},{2,3},{3,4},{4,5},{5,6},{6,7},{7,8},{8,9},{9,10},{10,1... | collective-permute-start | bytes 786440 | tf_op jit(solution)/shard_map/ppermute | solution.py:12
  18.4 1.2 copy-start.3
  20.6 178.1 %reduce-scatter.3.cloned.1.call-start = ((), (), s32[]{:S(2)}) async-start(), calls=%async_computation.2 | async-start | bytes 8912896 | tf_op jit(solution)/shard_map/reduce_scatter | solution.py:81
  28.6 12.1 %copy-start = (bf16[512,2,128]{2,1,0:T(2,128)(2,1)S(1)}, bf16[512,2,128]{2,1,0:T(2,128)(2,1)}, u32[]{:S(2)}) copy-start(bf16[512,2,128]{2,1,0:T(2,128)(2,1)} %param.10) | copy-start | bytes 786436
  28.6 12.1 %copy-start.12 = (bf16[2,128,128]{2,1,0:T(8,128)(2,1)S(1)}, bf16[2,128,128]{2,1,0:T(8,128)(2,1)}, u32[]{:S(2)}) copy-start(bf16[2,128,128]{2,1,0:T(8,128)(2,1)} %param.16) | copy-start | bytes 196612
  65.6 0.8 copy-start.14
  65.7 203.7 %all-gather.5.cloned.1.call-start = ((), (), s32[]{:S(2)}) async-start(), calls=%async_computation.5 | async-start | bytes 4456448 | tf_op jit(solution)/shard_map/all_gather | solution.py:57
  66.7 29.0 %copy-start.1 = (bf16[512,2,128]{2,1,0:T(2,128)(2,1)S(1)}, bf16[512,2,128]{2,1,0:T(2,128)(2,1)}, u32[]{:S(2)}) copy-start(bf16[512,2,128]{2,1,0:T(2,128)(2,1)} %param.9) | copy-start | bytes 786436
  66.7 45.3 %copy-start.9 = (bf16[2,128,256]{2,1,0:T(8,128)(2,1)S(1)}, bf16[2,128,256]{2,1,0:T(8,128)(2,1)}, u32[]{:S(2)}) copy-start(bf16[2,128,256]{2,1,0:T(8,128)(2,1)} %param.14) | copy-start | bytes 393220
  66.7 49.0 %copy-start.8 = (bf16[2,128,256]{2,1,0:T(8,128)(2,1)S(1)}, bf16[2,128,256]{2,1,0:T(8,128)(2,1)}, u32[]{:S(2)}) copy-start(bf16[2,128,256]{2,1,0:T(8,128)(2,1)} %param.13) | copy-start | bytes 393220
  95.9 18.0 %collective-permute-start.1 = (bf16[512,2,128]{2,1,0:T(2,128)(2,1)S(1)}, bf16[512,2,128]{2,1,0:T(2,128)(2,1)S(1)}, u32[]{:S(2)}, u32[]{:S(2)}) collective-permute-start(bf16[512,2,128]{2,1,0:T(2,128)(2,1)S(1)} %add_convert_fusion), channel_id=1, source_target_pairs={{0,1},{1,2},{2,3},{3,4},{4,5},{5,6},{6,7},{7,8},{8,9},{9,10},{10,1... | collective-permute-start | bytes 786440 | tf_op jit(solution)/shard_map/ppermute | solution.py:12
  115.0 0.7 copy-start.5
  204.7 176.9 %reduce-scatter.5.cloned.1.call-start = ((), (), s32[]{:S(2)}) async-start(), calls=%async_computation.4 | async-start | bytes 8912896 | tf_op jit(solution)/shard_map/reduce_scatter | solution.py:81
  207.1 12.2 %collective-permute-start.2 = (f32[512,2,128]{2,0,1:T(8,128)S(1)}, f32[512,2,128]{2,0,1:T(8,128)}, u32[]{:S(2)}, u32[]{:S(2)}) collective-permute-start(f32[512,2,128]{2,0,1:T(8,128)S(1)} %fusion.33), channel_id=1, source_target_pairs={{1,0},{2,1},{3,2},{4,3},{5,4},{6,5},{7,6},{8,7},{9,8},{10,9},{11,1... | collective-permute-start | bytes 1572872 | tf_op jit(solution)/shard_map/ppermute | solution.py:12
  247.1 1.0 copy-start.7
  247.1 1.2 copy-start.11
  247.1 3.1 copy-start.6
  247.1 399.1 %all-reduce.3.cloned.1.call-start = ((), (), s32[]{:S(2)}) async-start(), calls=%async_computation.6 | async-start | bytes 1572864 | tf_op jit(solution)/shard_map/psum | solution.py:116
  253.3 130.9 %copy-start.4 = (bf16[512,2,128]{2,1,0:T(2,128)(2,1)S(1)}, bf16[512,2,128]{2,1,0:T(2,128)(2,1)}, u32[]{:S(2)}) copy-start(bf16[512,2,128]{2,1,0:T(2,128)(2,1)} %copy-done.3) | copy-start | bytes 786436
  278.7 371.1 %copy-start.2 = (f32[512,2,128]{2,0,1:T(8,128)S(1)}, f32[512,2,128]{2,0,1:T(8,128)}, u32[]{:S(2)}) copy-start(f32[512,2,128]{2,0,1:T(8,128)} %get-tuple-element.27) | copy-start | bytes 1572868
  278.7 371.1 %copy-start.10 = (bf16[2,128,256]{2,1,0:T(8,128)(2,1)S(1)}, bf16[2,128,256]{2,1,0:T(8,128)(2,1)}, u32[]{:S(2)}) copy-start(bf16[2,128,256]{2,1,0:T(8,128)(2,1)} %param.14) | copy-start | bytes 393220
  279.7 106.4 %copy-start.13 = (f32[1,128,256]{2,1,0:T(8,128)S(1)}, f32[1,128,256]{2,1,0:T(8,128)}, u32[]{:S(2)}) copy-start(f32[1,128,256]{2,1,0:T(8,128)} %convolution_bitcast_fusion.2) | copy-start | bytes 393220
  387.2 262.6 %collective-permute-start.3 = (f32[512,2,128]{2,0,1:T(8,128)S(1)}, f32[512,2,128]{2,0,1:T(8,128)S(1)}, u32[]{:S(2)}, u32[]{:S(2)}) collective-permute-start(f32[512,2,128]{2,0,1:T(8,128)S(1)} %fusion.30), channel_id=1, source_target_pairs={{1,0},{2,1},{3,2},{4,3},{5,4},{6,5},{7,6},{8,7},{9,8},{10,9},{11,1... | collective-permute-start | bytes 1572872 | tf_op jit(solution)/shard_map/ppermute | solution.py:12
Sparse Core Ops, SparseCore 0:
  20.7 65.2 all-gather.2
  88.6 110.0 reduce-scatter.2
  204.8 64.4 all-gather.4
  271.8 109.7 reduce-scatter.4
  387.9 258.2 all-reduce.2
where the time goes:
time: 669 us; the launch traced here: 658 us
  waiting for transfers between devices  484 us (72%)
  matrix products  83.9 us (13%)
  starting transfers between devices  26.1 us (4%)
  local copies, waits for them, and re-layouts  25.1 us (4%)
  between operations  21 us (3%)
  other arithmetic  18.5 us (3%)
    psum x1, waiting for transfers between devices, per_device(): lax.psum((jnp.stack(outs_prev[::-1]), jnp.stack(outs_cur[::-1]), jnp.stac...  254 us
    reduce_scatter x2, waiting for transfers between devices, per_device(): lax.psum_scatter(lax.dot_general(row_matrix, gdiff_rows, (((0,), (0,)), (...  185 us
    dot_general x2, matrix products, per_device(): lax.dot_general(row_matrix, gdiff_rows, (((0,), (0,)), ((), ())), preferr...  48.8 us
    all_gather x2, waiting for transfers between devices, per_device(): lax.all_gather(gated.reshape(rows, time_days * width), 'firm', axis=0, ti...  35.4 us
    ppermute x4, starting transfers between devices, shifted(): return lax.ppermute(array, axis, pairs)  25.6 us
    dot_general x2, matrix products, folder(): return jnp.dot(matrix, piece, preferred_element_type=jnp.float32)  18.6 us
  transfers between devices with their start and end apart: 9, of which 7 were waited for; matrix products, arithmetic and copies ran while one was open for 16% of the time, Pallas kernels for 0%

commit v1 on v0

--- a/solution.py
+++ b/solution.py
@@ -54,7 +54,15 @@
         gated = (jnp.tanh(filt) * jax.nn.sigmoid(gate)).astype(jnp.bfloat16)
         diffused = folder(
             row_matrix,
-            lax.all_gather(gated.reshape(rows, time_days * width), "firm", axis=0, tiled=True),
+            jnp.concatenate(
+                lax.all_to_all(
+                    jnp.stack([gated.reshape(rows, time_days * width)] * lax.axis_size("firm")),
+                    "firm",
+                    0,
+                    0,
+                ),
+                axis=0,
+            ),
         ).astype(jnp.bfloat16)
         mixed = jnp.dot(gated, w_self[layer_index], preferred_element_type=jnp.float32)
         mixed = mixed + jnp.dot(

time: 669 us -> 763 us (1.14)
  waiting for transfers between devices: 484 us -> 572 us
  starting transfers between devices: 26.1 us -> 34.3 us
    all_to_all x0 -> x2, waiting for transfers between devices: none -> 243 us  [per_device(): lax.all_to_all(jnp.stack([gated.reshape(rows, time_days * width)] * lax.a...]
    reduce_scatter x2, waiting for transfers between devices: 185 us -> 58.7 us  [per_device(): lax.psum_scatter(lax.dot_general(row_matrix, gdiff_rows, (((0,), (0,)), (...]
    all_gather x2 -> x0, waiting for transfers between devices: 35.4 us -> none  [per_device(): lax.all_gather(gated.reshape(rows, time_days * width), 'firm', axis=0, ti...]
    all_to_all x0 -> x2, starting transfers between devices: none -> 16.1 us  [per_device(): lax.all_to_all(jnp.stack([gated.reshape(rows, time_days * width)] * lax.a...]
    ppermute x4, starting transfers between devices: 25.6 us -> 17.9 us  [shifted(): return lax.ppermute(array, axis, pairs)]
  transfers between devices with their start and end apart: 9 -> 9, of which waited for: 7 -> 8; matrix products, arithmetic and copies ran while one was open for 16% -> 5% of each run, Pallas kernels for 0% -> 0%
where the time goes in v1:
time: 763 us; the launch traced here: 754 us
  waiting for transfers between devices  572 us (75%)
  matrix products  83.2 us (11%)
  starting transfers between devices  34.3 us (4%)
  local copies, waits for them, and re-layouts  25.1 us (3%)
  between operations  21 us (3%)
  other arithmetic  17.5 us (2%)
    psum x1, waiting for transfers between devices, per_device(): lax.psum((jnp.stack(outs_prev[::-1]), jnp.stack(outs_cur[::-1]), jnp.stac...  261 us
    all_to_all x2, waiting for transfers between devices, per_device(): lax.all_to_all(jnp.stack([gated.reshape(rows, time_days * width)] * lax.a...  243 us
    reduce_scatter x2, waiting for transfers between devices, per_device(): lax.psum_scatter(lax.dot_general(row_matrix, gdiff_rows, (((0,), (0,)), (...  58.7 us
    dot_general x2, matrix products, per_device(): lax.dot_general(row_matrix, gdiff_rows, (((0,), (0,)), ((), ())), preferr...  48.7 us
    dot_general x2, matrix products, folder(): return jnp.dot(matrix, piece, preferred_element_type=jnp.float32)  18.9 us
    ppermute x4, starting transfers between devices, shifted(): return lax.ppermute(array, axis, pairs)  17.9 us
    all_to_all x2, starting transfers between devices, per_device(): lax.all_to_all(jnp.stack([gated.reshape(rows, time_days * width)] * lax.a...  16.1 us
  transfers between devices with their start and end apart: 9, of which 8 were waited for; matrix products, arithmetic and copies ran while one was open for 5% of the time, Pallas kernels for 0%

profile of v1, /device:TPU:97, one launch (start us, length us, event | category | flops | bytes accessed | tf_op | source)
XLA Modules:
  0.0 753.7 jit_solution(4745843494310478073)
XLA Ops:
  7.9 7.2 multiply_bitcast_fusion
  15.1 12.1 %copy.22 = bf16[4,128,64,128]{3,2,1,0:T(8,128)(2,1)} copy(bf16[4,128,64,128]{3,1,2,0:T(8,128)(2,1)} %multiply_bitcast_fusion) | data formatting | bytes 16777216 | tf_op jit(solution)/shard_map/transpose | solution.py:38
  27.6 24.5 %fusion.6 = f32[8192,256]{1,0:T(8,128)} fusion(bf16[512,256]{1,0:T(8,128)(2,1)S(1)} %reshape.90, bf16[64,8,64,128]{3,2,1,0:T(8,128)(2,1)} %bitcast.126), kind=kOutput, calls=%fused_computation.6 | convolution fusion | flops 2147483648 | bytes 17039360 | tf_op jit(solution)/shard_map/dot_general | solution.py:90
  53.1 5.4 collective-permute-start
  64.0 2.4 stack.42
  66.5 7.2 all-to-all-start
  74.0 127.2 %all-to-all-done = bf16[16,512,256]{2,1,0:T(8,128)(2,1)} async-done(((bf16[16,512,256]{2,1,0:T(8,128)(2,1)}), bf16[16,512,256]{2,1,0:T(8,128)(2,1)}, u32[]{:S(2)}, u32[]{:S(2)}) %all-to-all-start) | async-done | bytes 4194336 | tf_op jit(solution)/shard_map/all_to_all | solution.py:58
  201.2 9.4 %fusion.13 = bf16[512,256]{1,0:T(8,128)(2,1)S(1)} fusion(bf16[8192,256]{1,0:T(8,128)(2,1)} %bitcast.10, bf16[64,8,64,128]{3,2,1,0:T(8,128)(2,1)} %bitcast.127), kind=kOutput, calls=%fused_computation.23 | convolution fusion | flops 2147614720 | bytes 12845056 | tf_op jit(solution)/shard_map/dot_general | solution.py:30
  211.2 7.4 collective-permute-start.1
  224.1 19.6 %reduce-scatter.3.cloned.1.call-done = f32[512,256]{1,0:T(8,128)} async-done(((f32[8192,256]{1,0:T(8,128)}), f32[512,256]{1,0:T(8,128)}) %reduce-scatter.3.cloned.1.call-update) | async-done | bytes 524304 | tf_op jit(solution)/shard_map/reduce_scatter | solution.py:89
  244.8 2.4 multiply_convert_fusion.3
  248.2 2.8 collective-permute-start.2
  253.0 7.5 collective-permute-done.2
  260.4 2.2 fusion.68
  264.0 24.1 %fusion.2 = f32[8192,256]{1,0:T(8,128)} fusion(bf16[512,256]{1,0:T(8,128)(2,1)S(1)} %reshape.100, bf16[64,8,64,128]{3,2,1,0:T(8,128)(2,1)} %bitcast.128), kind=kOutput, calls=%fused_computation.2 | convolution fusion | flops 2147483648 | bytes 17039360 | tf_op jit(solution)/shard_map/dot_general | solution.py:90
  289.2 2.4 stack.53
  291.6 8.8 %all-to-all-start.1 = ((bf16[16,512,256]{2,1,0:T(8,128)(2,1)}), bf16[16,512,256]{2,1,0:T(8,128)(2,1)}, u32[]{:S(2)}, u32[]{:S(2)}) async-start(bf16[16,512,256]{2,1,0:T(8,128)(2,1)} %stack.53), calls=%async_computation.3 | async-start | bytes 8388608 | tf_op jit(solution)/shard_map/all_to_all | solution.py:58
  301.0 1.9 convolution_bitcast_fusion
  302.9 1.9 convolution_bitcast_fusion.2
  306.0 115.5 %all-to-all-done.1 = bf16[16,512,256]{2,1,0:T(8,128)(2,1)} async-done(((bf16[16,512,256]{2,1,0:T(8,128)(2,1)}), bf16[16,512,256]{2,1,0:T(8,128)(2,1)}, u32[]{:S(2)}, u32[]{:S(2)}) %all-to-all-start.1) | async-done | bytes 4194336 | tf_op jit(solution)/shard_map/all_to_all | solution.py:58
  421.5 9.5 %fusion.16 = bf16[512,256]{1,0:T(8,128)(2,1)S(1)} fusion(bf16[8192,256]{1,0:T(8,128)(2,1)} %bitcast.35, bf16[64,8,64,128]{3,2,1,0:T(8,128)(2,1)} %bitcast.129), kind=kOutput, calls=%fused_computation.24 | convolution fusion | flops 2147614720 | bytes 12845056 | tf_op jit(solution)/shard_map/dot_general | solution.py:30
  432.0 39.1 %reduce-scatter.5.cloned.1.call-done = f32[512,256]{1,0:T(8,128)} async-done(((f32[8192,256]{1,0:T(8,128)}), f32[512,256]{1,0:T(8,128)}) %reduce-scatter.5.cloned.1.call-update) | async-done | bytes 524304 | tf_op jit(solution)/shard_map/reduce_scatter | solution.py:89
  476.7 2.3 collective-permute-start.3
  480.9 260.7 %all-reduce.3.cloned.1.call-done = (f32[2,128,256]{2,1,0:T(8,128)}, f32[2,128,256]{2,1,0:T(8,128)}, f32[2,128,128]{2,1,0:T(8,128)}, f32[2,128,128]{2,1,0:T(8,128)}) async-done(((f32[2,128,256]{2,1,0:T(8,128)}, f32[2,128,256]{2,1,0:T(8,128)}, f32[2,128,128]{2,1,0:T(8,128)}, f32[2,128,128]{2,1,0:T(8,128)}), (f32[2,128,256]{2,1,0:T(8,128)}, f32[2,128,256]{2,1,0:T(8,128)}, f32[2,128,128]{2,1,0:T(8,128)}, ...) | async-done | bytes 786448 | tf_op jit(solution)/shard_map/psum | solution.py:124
  (89 shorter events, 29.0 us)
Async XLA Ops:
  7.2 236.6 %reduce-scatter.3.cloned.1.call-start = ((), (), s32[]{:S(2)}) async-start(), calls=%async_computation.4 | async-start | bytes 8912896 | tf_op jit(solution)/shard_map/reduce_scatter | solution.py:89
  15.1 12.1 %copy-start = (bf16[512,2,128]{2,1,0:T(2,128)(2,1)S(1)}, bf16[512,2,128]{2,1,0:T(2,128)(2,1)}, u32[]{:S(2)}) copy-start(bf16[512,2,128]{2,1,0:T(2,128)(2,1)} %param.10) | copy-start | bytes 786436
  15.1 12.1 %copy-start.14 = (bf16[2,128,128]{2,1,0:T(8,128)(2,1)S(1)}, bf16[2,128,128]{2,1,0:T(8,128)(2,1)}, u32[]{:S(2)}) copy-start(bf16[2,128,128]{2,1,0:T(8,128)(2,1)} %param.16) | copy-start | bytes 196612
  52.1 0.9 copy-start.1
  52.2 6.3 copy-start.17
  52.2 8.2 %copy-start.9 = (bf16[2,128,256]{2,1,0:T(8,128)(2,1)S(1)}, bf16[2,128,256]{2,1,0:T(8,128)(2,1)}, u32[]{:S(2)}) copy-start(bf16[2,128,256]{2,1,0:T(8,128)(2,1)} %param.14) | copy-start | bytes 393220
  52.2 11.3 %copy-start.8 = (bf16[2,128,256]{2,1,0:T(8,128)(2,1)S(1)}, bf16[2,128,256]{2,1,0:T(8,128)(2,1)}, u32[]{:S(2)}) copy-start(bf16[2,128,256]{2,1,0:T(8,128)(2,1)} %param.13) | copy-start | bytes 393220
  53.1 8.7 %collective-permute-start = (bf16[512,2,128]{2,1,0:T(2,128)(2,1)S(1)}, bf16[512,2,128]{2,1,0:T(2,128)(2,1)S(1)}, u32[]{:S(2)}, u32[]{:S(2)}) collective-permute-start(bf16[512,2,128]{2,1,0:T(2,128)(2,1)S(1)} %copy-done.1), channel_id=1, source_target_pairs={{0,1},{1,2},{2,3},{3,4},{4,5},{5,6},{6,7},{7,8},{8,9},{9,10},{10,1... | collective-permute-start | bytes 786440 | tf_op jit(solution)/shard_map/ppermute | solution.py:12
  63.4 10.3 %copy-start.16 = (bf16[2,128,128]{2,1,0:T(8,128)(2,1)S(1)}, bf16[2,128,128]{2,1,0:T(8,128)(2,1)}, u32[]{:S(2)}) copy-start(bf16[2,128,128]{2,1,0:T(8,128)(2,1)} %param.15) | copy-start | bytes 196612
  66.5 134.7 %all-to-all-start = ((bf16[16,512,256]{2,1,0:T(8,128)(2,1)}), bf16[16,512,256]{2,1,0:T(8,128)(2,1)}, u32[]{:S(2)}, u32[]{:S(2)}) async-start(bf16[16,512,256]{2,1,0:T(8,128)(2,1)} %stack.42), calls=%async_computation.1 | async-start | bytes 8388608 | tf_op jit(solution)/shard_map/all_to_all | solution.py:58
  73.7 397.4 %reduce-scatter.5.cloned.1.call-start = ((), (), s32[]{:S(2)}) async-start(), calls=%async_computation.5 | async-start | bytes 8912896 | tf_op jit(solution)/shard_map/reduce_scatter | solution.py:89
  211.2 10.7 %collective-permute-start.1 = (bf16[512,2,128]{2,1,0:T(2,128)(2,1)S(1)}, bf16[512,2,128]{2,1,0:T(2,128)(2,1)S(1)}, u32[]{:S(2)}, u32[]{:S(2)}) collective-permute-start(bf16[512,2,128]{2,1,0:T(2,128)(2,1)S(1)} %add_convert_fusion), channel_id=1, source_target_pairs={{0,1},{1,2},{2,3},{3,4},{4,5},{5,6},{6,7},{7,8},{8,9},{9,10},{10,1... | collective-permute-start | bytes 786440 | tf_op jit(solution)/shard_map/ppermute | solution.py:12
  222.9 24.3 %copy-start.5 = (bf16[512,2,128]{2,1,0:T(2,128)(2,1)}, bf16[512,2,128]{2,1,0:T(2,128)(2,1)S(1)}, u32[]{:S(2)}) copy-start(bf16[512,2,128]{2,1,0:T(2,128)(2,1)S(1)} %fusion.28) | copy-start | bytes 786436
  247.2 1.0 copy-start.13
  248.2 12.2 %collective-permute-start.2 = (f32[512,2,128]{2,0,1:T(8,128)S(1)}, f32[512,2,128]{2,0,1:T(8,128)}, u32[]{:S(2)}, u32[]{:S(2)}) collective-permute-start(f32[512,2,128]{2,0,1:T(8,128)S(1)} %fusion.33), channel_id=1, source_target_pairs={{1,0},{2,1},{3,2},{4,3},{5,4},{6,5},{7,6},{8,7},{9,8},{10,9},{11,1... | collective-permute-start | bytes 1572872 | tf_op jit(solution)/shard_map/ppermute | solution.py:12
  288.2 14.7 %copy-start.6 = (bf16[512,2,128]{2,1,0:T(2,128)(2,1)S(1)}, bf16[512,2,128]{2,1,0:T(2,128)(2,1)}, u32[]{:S(2)}) copy-start(bf16[512,2,128]{2,1,0:T(2,128)(2,1)} %copy-done.5) | copy-start | bytes 786436
  291.6 9.4 %copy-start.12 = (bf16[1024,128]{1,0:T(8,128)(2,1)S(1)}, bf16[1024,128]{1,0:T(8,128)(2,1)}, u32[]{:S(2)}) copy-start(bf16[1024,128]{1,0:T(8,128)(2,1)} %copy-done.11) | copy-start | bytes 786436
  291.6 129.9 %all-to-all-start.1 = ((bf16[16,512,256]{2,1,0:T(8,128)(2,1)}), bf16[16,512,256]{2,1,0:T(8,128)(2,1)}, u32[]{:S(2)}, u32[]{:S(2)}) async-start(bf16[16,512,256]{2,1,0:T(8,128)(2,1)} %stack.53), calls=%async_computation.3 | async-start | bytes 8388608 | tf_op jit(solution)/shard_map/all_to_all | solution.py:58
  300.4 441.2 %all-reduce.3.cloned.1.call-start = ((), (), s32[]{:S(2)}) async-start(), calls=%async_computation.6 | async-start | bytes 1572864 | tf_op jit(solution)/shard_map/psum | solution.py:124
  421.5 52.2 %copy-start.4 = (bf16[512,2,128]{2,1,0:T(2,128)(2,1)S(1)}, bf16[512,2,128]{2,1,0:T(2,128)(2,1)}, u32[]{:S(2)}) copy-start(bf16[512,2,128]{2,1,0:T(2,128)(2,1)} %copy-done.3) | copy-start | bytes 786436
  431.0 314.2 %copy-start.2 = (f32[512,2,128]{2,0,1:T(8,128)S(1)}, f32[512,2,128]{2,0,1:T(8,128)}, u32[]{:S(2)}) copy-start(f32[512,2,128]{2,0,1:T(8,128)} %get-tuple-element.27) | copy-start | bytes 1572868
  431.0 314.2 %copy-start.10 = (bf16[2,128,256]{2,1,0:T(8,128)(2,1)S(1)}, bf16[2,128,256]{2,1,0:T(8,128)(2,1)}, u32[]{:S(2)}) copy-start(bf16[2,128,256]{2,1,0:T(8,128)(2,1)} %param.14) | copy-start | bytes 393220
  432.0 43.6 %copy-start.15 = (f32[1,128,256]{2,1,0:T(8,128)S(1)}, f32[1,128,256]{2,1,0:T(8,128)}, u32[]{:S(2)}) copy-start(f32[1,128,256]{2,1,0:T(8,128)} %convolution_bitcast_fusion.2) | copy-start | bytes 393220
  476.7 268.5 %collective-permute-start.3 = (f32[512,2,128]{2,0,1:T(8,128)S(1)}, f32[512,2,128]{2,0,1:T(8,128)S(1)}, u32[]{:S(2)}, u32[]{:S(2)}) collective-permute-start(f32[512,2,128]{2,0,1:T(8,128)S(1)} %fusion.30), channel_id=1, source_target_pairs={{1,0},{2,1},{3,2},{4,3},{5,4},{6,5},{7,6},{8,7},{9,8},{10,9},{11,1... | collective-permute-start | bytes 1572872 | tf_op jit(solution)/shard_map/ppermute | solution.py:12
  (3 other events, 2.3 us)
Sparse Core Ops, SparseCore 0:
  52.3 191.3 reduce-scatter.2
  288.3 182.7 reduce-scatter.4
  477.6 264.0 all-reduce.2
